TPU v7x, 32 devices: a whole 2x2x4 slice. The times are simulated.
32 devices in a mesh: dp: 8 (over z, y), tensor: 4 (over x, core).
Axes of the slice: x: 2, y: 2, z: 4, core: 2. Of those that a mesh axis runs over, the one named last changes fastest.
Arguments:
- tree_ids: int32 [8, 64], P('dp'), may hold values from 0 to 65535, as said below
- ancestors: int32 [8, 64, 64], P('dp'), may hold values from 0 to 1, as said below
- lengths: int32 [8], P('dp'), may hold values from 64 to 1024, as said below
- table: bfloat16 [65536, 4096], P('dp', 'tensor'), may hold values from -3 to 3
- gain: bfloat16 [4096], replicated, may hold values from 0.25 to 1.75
- w_query: bfloat16 [4096, 4096], P(None, 'tensor'), may hold values from -0.09375 to 0.09375
- w_kv: bfloat16 [2, 4096, 1024], P(None, None, 'tensor'), may hold values from -0.09375 to 0.09375
- w_out: bfloat16 [4096, 4096], P('tensor'), may hold values from -0.09375 to 0.09375
- key_cache: bfloat16 [8, 8, 1024, 128], P('dp', 'tensor'), may hold values from -480 to 480
- value_cache: bfloat16 [8, 8, 1024, 128], P('dp', 'tensor'), may hold values from -6 to 6
Outputs:
- layer_output: bfloat16 [512, 4096], P('dp', 'tensor')
Inputs may be any that keep to these rules, and one draw needn't show every extreme that they name: `tree_ids`: split the vocabulary into equal consecutive parts, one for each index of dp; of the nodes of the rows of one index of dp, at most 16 have ids in any one part, and exactly 16 in some part. Row n of each row's matrix marks node n and all its ancestors in that row's tree; node 0 is the root and every other node's parent has a smaller index. `lengths`: some row has all 1024 slots live.
All inputs are finite; a program needn't handle non-finite values.
Results may differ from a plain program's by a relative error of at most 0.004.
The roundings to bfloat16 on the way count: a program that leaves them out, or rounds other values in their place, can miss the bound.
Values may be sent and summed in bfloat16 or wider, within the bound.
A program may use at most 128 MiB of HBM per device.

v0:
```python
import math

import jax
import jax.numpy as jnp
from jax import lax
from jax.sharding import PartitionSpec as P

D = 4096


EPS = 1e-05
NEG = -1e30
THETA = 500000.0


def rotary(values, positions):
    half_dim = values.shape[-1] // 2
    freq_index = jnp.arange(half_dim, dtype=jnp.float32)
    inverse = jnp.exp(freq_index * (-2.0 * math.log(THETA) / values.shape[-1]))
    angles = positions[:, None] * inverse[None, :]
    cosine = jnp.cos(angles)[:, None, :]
    sine_part = jnp.sin(angles)[:, None, :]
    lower_half = values[..., :half_dim]
    upper_half = values[..., half_dim:]
    return jnp.concatenate(
        [
            lower_half * cosine - upper_half * sine_part,
            upper_half * cosine + lower_half * sine_part,
        ],
        axis=-1,
    )


def contract(left_side, right_side):
    return lax.dot_general(
        left_side, right_side, (((1,), (1,)), ((), ())), preferred_element_type=jnp.float32
    )


def to_groups(tensor_in, kv_heads, head_dim):
    row_count, node_count, width_all = tensor_in.shape
    per_group = width_all // (kv_heads * head_dim)
    grouped = tensor_in.reshape(row_count, node_count, kv_heads, per_group, head_dim).transpose(
        0, 2, 3, 1, 4
    )
    return grouped.reshape(row_count, kv_heads, per_group * node_count, head_dim)


def from_groups(tensor_in, node_count):
    row_count, kv_heads, group_rows, head_dim = tensor_in.shape
    grouped = tensor_in.reshape(row_count, kv_heads, group_rows // node_count, node_count, head_dim)
    return grouped.transpose(0, 3, 1, 2, 4).reshape(row_count, node_count, -1)


def attend(query_group, keys_tree, values_tree, keys_cache, values_cache, live_len, tree_mask):
    score_scale = keys_cache.shape[-1] ** (-0.5)
    slot_count = keys_cache.shape[0]
    cache_scores = contract(query_group, keys_cache) * score_scale
    columns = jnp.arange(slot_count, dtype=jnp.int32)
    cache_scores = jnp.where(columns[None, :] < live_len, cache_scores, NEG)
    tree_scores = contract(query_group, keys_tree) * score_scale
    groups = query_group.shape[0] // tree_mask.shape[0]
    tree_scores = jnp.where(jnp.tile(tree_mask, (groups, 1)) > 0, tree_scores, NEG)
    row_top = jnp.maximum(jnp.max(cache_scores, axis=1), jnp.max(tree_scores, axis=1))[:, None]
    cache_exp = jnp.exp(cache_scores - row_top)
    tree_exp = jnp.exp(tree_scores - row_top)
    denominator = jnp.sum(cache_exp, axis=1) + jnp.sum(tree_exp, axis=1)
    cache_weights = cache_exp.astype(jnp.bfloat16)
    weighted = jnp.dot(
        tree_exp.astype(jnp.bfloat16), values_tree, preferred_element_type=jnp.float32
    )
    weighted = weighted + jnp.dot(cache_weights, values_cache, preferred_element_type=jnp.float32)
    return (weighted / denominator[:, None]).astype(jnp.bfloat16)


def slot_ranks(owner_blocks):
    token_span = owner_blocks.shape[-1]
    positions_here = jnp.arange(token_span, dtype=jnp.int32)
    earlier = positions_here[None, :] < positions_here[:, None]
    same_owner = owner_blocks[..., :, None] == owner_blocks[..., None, :]
    return jnp.sum((same_owner & earlier).astype(jnp.int32), axis=-1)


def shards(tree_ids, ancestors, lengths, table, gain, w_query, w_kv, w_out, key_cache, value_cache):
    row_count, node_count = tree_ids.shape
    token_count = row_count * node_count
    head_dim = key_cache.shape[3]
    kv_local = key_cache.shape[1]
    all_ids = lax.all_gather(tree_ids, "dp", axis=0, tiled=True).reshape(-1)
    vocab_rows = table.shape[0]
    dp_count = lax.axis_size("dp")
    my_index = lax.axis_index("dp")
    capacity = 2 * ((token_count + dp_count - 1) // dp_count)
    block_ids = all_ids.reshape(dp_count, token_count)
    owner_blocks = block_ids // vocab_rows
    ranks = slot_ranks(owner_blocks)
    mine = owner_blocks == my_index
    slot_hit = mine[:, :, None] & (
        ranks[:, :, None] == jnp.arange(capacity, dtype=jnp.int32)[None, None, :]
    )
    token_place = jnp.arange(token_count, dtype=jnp.int32)[None, :, None]
    source_token = jnp.sum(jnp.where(slot_hit, token_place, 0), axis=1)
    slot_used = jnp.any(slot_hit, axis=1)
    source_ids = jnp.take_along_axis(block_ids, source_token, axis=1)
    source_offsets = jnp.clip(source_ids - my_index * vocab_rows, 0, vocab_rows - 1)
    slot_rows = jnp.take(table, source_offsets.reshape(-1), axis=0).reshape(
        dp_count, capacity, table.shape[1]
    )
    slot_rows = jnp.where(slot_used[:, :, None], slot_rows, jnp.zeros((), slot_rows.dtype))
    arrived = lax.all_to_all(slot_rows, "dp", split_axis=0, concat_axis=0, tiled=True)
    own_ids = tree_ids.reshape(-1)
    own_owner = own_ids // vocab_rows
    own_rank = slot_ranks(own_owner)
    flat_slot = own_owner * capacity + own_rank
    embedded = jnp.take(arrived.reshape(dp_count * capacity, table.shape[1]), flat_slot, axis=0)
    gain_full = gain.astype(jnp.float32)
    features = lax.all_gather(embedded, "tensor", axis=1, tiled=True).astype(jnp.float32)
    inv_rms = lax.rsqrt(jnp.sum(features * features, axis=1) / D + EPS)
    normed = (features * inv_rms[:, None] * gain_full[None, :]).astype(jnp.bfloat16)
    queries = jnp.dot(normed, w_query, preferred_element_type=jnp.float32)
    keys_new = jnp.dot(normed, w_kv[0], preferred_element_type=jnp.float32)
    values_raw = jnp.dot(normed, w_kv[1], preferred_element_type=jnp.float32)
    values_new = values_raw.astype(jnp.bfloat16).reshape(row_count, node_count, -1)
    node_depth = jnp.sum(ancestors, axis=2) - 1
    positions = (lengths[:, None] + node_depth).reshape(-1).astype(jnp.float32)
    query_heads = w_query.shape[1] // head_dim
    queries = rotary(queries.reshape(token_count, query_heads, head_dim), positions).astype(
        jnp.bfloat16
    )
    queries = queries.reshape(row_count, node_count, query_heads * head_dim)
    keys_new = rotary(keys_new.reshape(token_count, kv_local, head_dim), positions).astype(
        jnp.bfloat16
    )
    keys_new = keys_new.reshape(row_count, node_count, kv_local * head_dim)
    query_groups = to_groups(queries, kv_local, head_dim)
    key_groups = to_groups(keys_new, kv_local, head_dim)
    value_groups = to_groups(values_new, kv_local, head_dim)

    def per_row(row_items):
        row_q, row_k, row_v, row_kc, row_vc, live_len, tree_mask = row_items

        def per_head(head_items):
            return attend(
                head_items[0],
                head_items[1],
                head_items[2],
                head_items[3],
                head_items[4],
                live_len,
                tree_mask,
            )

        return lax.map(per_head, (row_q, row_k, row_v, row_kc, row_vc))

    contexts = lax.map(
        per_row,
        (query_groups, key_groups, value_groups, key_cache, value_cache, lengths, ancestors),
    )
    contexts = from_groups(contexts, node_count).reshape(token_count, query_heads * head_dim)
    partial_out = jnp.dot(contexts, w_out, preferred_element_type=jnp.float32)
    attention = lax.psum_scatter(partial_out, "tensor", scatter_dimension=1, tiled=True)
    return (embedded.astype(jnp.float32) + attention).astype(jnp.bfloat16)


def solution(mesh):
    in_specs = (
        P("dp", None),
        P("dp", None, None),
        P("dp"),
        P("dp", "tensor"),
        P(),
        P(None, "tensor"),
        P(None, None, "tensor"),
        P("tensor", None),
        P("dp", "tensor", None, None),
        P("dp", "tensor", None, None),
    )
    out_specs = P("dp", "tensor")
    return jax.shard_map(shards, mesh=mesh, in_specs=in_specs, out_specs=out_specs, check_vma=False)
```

profile of v0, /device:TPU:0, one launch (start us, length us, event | category | flops | bytes accessed | tf_op | source)
XLA Modules:
  0.0 113.7 jit_solution(4923900093917061358)
XLA Ops:
  6.5 0.0 copy-start.4
  6.5 22.5 %all-gather = s32[8,1,64]{2,1,0:T(1,128)S(1)} all-gather(s32[1,1,64]{2,1,0:T(1,128)} %bitcast.147), channel_id=1, replica_groups=mesh['dp'=8,'tensor'=4] {'dp'}, dimensions={0}, use_global_device_ids=true | all-gather | bytes 2304 | tf_op jit(solution)/shard_map/all_gather | solution.py:89
  29.0 0.3 convert_reduce_fusion
  29.4 0.2 select_reduce_fusion
  29.6 0.1 reduce_sum.73
  29.7 0.2 fusion.43
  29.9 0.1 reshape.421
  30.0 1.0 gather_fusion.2
  31.0 0.0 copy-start.2
  31.0 0.0 copy-start.3
  31.0 0.1 reshape.424
  31.1 9.0 %gather_fusion = bf16[128,1024]{1,0:T(8,128)(2,1)S(1)} fusion(bf16[8192,1024]{1,0:T(8,128)(2,1)} %param.15, s32[1024]{0:T(1024)S(1)} %pad_clamp_fusion.1), kind=kCustom, calls=%fused_computation | custom fusion | bytes 524800 | tf_op jit(solution)/shard_map/jit(_take)/gather | solution.py:106
  40.1 0.8 select_select_fusion
  41.0 3.4 %all-to-all-start = ((bf16[8,16,1024]{2,1,0:T(8,128)(2,1)}), bf16[8,16,1024]{2,1,0:T(8,128)(2,1)S(1)}, u32[]{:S(2)}, u32[]{:S(2)}) async-start(bf16[8,16,1024]{2,1,0:T(8,128)(2,1)} %select_select_fusion), calls=%async_computation | async-start | bytes 524288 | tf_op jit(solution)/shard_map/all_to_all | solution.py:110
  44.4 0.0 reduce-scatter.2.cloned.1.call-start
  44.4 0.0 copy-done.4
  44.5 0.2 convert_reduce_fusion.1
  44.7 3.1 %slice_bitcast_fusion = bf16[256,4096]{0,1:T(8,128)(2,1)} fusion(bf16[2,4096,256]{2,1,0:T(8,128)(2,1)} %param.18), kind=kLoop, calls=%fused_computation.42 | loop fusion | bytes 4194304 | tf_op jit(solution)/shard_map/dot_general | solution.py:121
  48.4 0.0 copy-done.2
  48.4 0.1 reduce_sum.76
  48.6 0.1 copy.29
  48.6 0.0 copy-done.3
  48.7 2.9 %copy.32 = bf16[256,4096]{1,0:T(8,128)(2,1)S(1)} copy(bf16[256,4096]{0,1:T(8,128)(2,1)} %slice_bitcast_fusion) | data formatting | bytes 4194304 | tf_op jit(solution)/shard_map/dot_general | solution.py:121
  51.6 0.2 multiply_cosine_fusion
  51.8 0.7 all-to-all-done
  52.5 0.7 gather_fusion.1
  53.2 0.1 broadcast_select_fusion
  53.3 7.2 %all_gather.7 = bf16[64,4096]{1,0:T(8,128)(2,1)S(1)} all-gather(bf16[64,1024]{1,0:T(8,128)(2,1)S(1)} %broadcast_select_fusion), channel_id=1, replica_groups=mesh['dp'=8,'tensor'=4] {'tensor'}, dimensions={1}, use_global_device_ids=true | all-gather | bytes 655360 | tf_op jit(solution)/shard_map/all_gather | solution.py:117
  60.5 0.2 fusion.37
  60.7 2.1 %fusion.34 = bf16[64,256]{1,0:T(8,128)(2,1)S(1)} fusion(bf16[2,4096,256]{2,1,0:T(8,128)(2,1)} %param.18, bf16[64,4096]{1,0:T(8,128)(2,1)S(1)} %all_gather.7, f32[4096]{0:T(1024)S(1)} %convert_element_type.60, f32[64]{0:T(128)S(1)} %add_rsqrt_fusion), kind=kOutput, calls=%fused_computation.46 | convolution fusion | flops 135282688 | bytes 2670848 | tf_op jit(solution)/shard_map/dot_general | solution.py:122
  62.8 0.8 fusion.40
  63.6 0.0 copy-start
  63.6 0.0 copy-start.1
  63.7 5.1 %convolution_bitcast_fusion = f32[8,8,8,128]{3,1,2,0:T(8,128)S(1)} fusion(bf16[4096,1024]{1,0:T(8,128)(2,1)} %param.17, bf16[64,4096]{1,0:T(8,128)(2,1)S(1)} %all_gather.7, f32[4096]{0:T(1024)S(1)} %convert_element_type.60, f32[64]{0:T(128)S(1)} %add_rsqrt_fusion), kind=kOutput, calls=%fused_computation.45 | convolution fusion | flops 537919488 | bytes 9191680 | tf_op jit(solution)/shard_map/dot_general | solution.py:120
  68.8 0.1 fusion.44
  68.9 0.2 subtract_convert_fusion
  69.1 0.1 pad_maximum_fusion
  69.2 0.1 maximum_bitcast_fusion
  69.3 0.0 copy-done
  69.3 0.0 copy-done.1
  69.4 4.8 %while.17 = (s32[]{:T(128)}, bf16[2,256,128]{2,1,0:T(8,128)(2,1)S(1)}, s32[64,64]{0,1:T(8,128)S(1)}, bf16[2,256,128]{2,1,0:T(8,128)(2,1)S(1)}, bf16[2,64,128]{2,...) while((s32[]{:T(128)}, ...), condition=%wide.region_11.12_spmd, body=%wide.region_6.11_spmd.sunk | while | flops 144658944 | bytes 4468845 | solution.py:153
  69.4 0.7 iota_compare_fusion.4
  70.0 0.4 fusion.79
  70.5 0.1 gt.11
  70.6 0.2 fusion.78
  70.8 0.3 fusion.81
  71.1 0.2 fusion.80
  71.3 0.4 fusion.83
  71.7 0.7 iota_compare_fusion.4
  72.4 0.4 fusion.79
  72.8 0.1 gt.11
  73.0 0.2 fusion.78
  73.2 0.3 fusion.81
  73.5 0.2 fusion.80
  73.7 0.4 fusion.83
  74.1 0.1 copy.38
  74.2 0.1 reshape_reshape.9
  74.3 5.9 %fusion.59 = f32[64,4096]{1,0:T(8,128)} fusion(bf16[64,1024]{1,0:T(8,128)(2,1)S(1)} %reshape_reshape.9, bf16[1024,4096]{1,0:T(8,128)(2,1)} %param.19), kind=kOutput, calls=%fused_computation.120 | convolution fusion | flops 536870912 | bytes 9568256 | tf_op jit(solution)/shard_map/dot_general | solution.py:160
  80.2 0.0 reduce-scatter.2.cloned.1.call-update
  80.3 24.9 %reduce-scatter.2.cloned.1.call-done = f32[64,1024]{1,0:T(8,128)} async-done(((f32[64,4096]{1,0:T(8,128)}), f32[64,1024]{1,0:T(8,128)}) %reduce-scatter.2.cloned.1.call-update) | async-done | bytes 262160 | tf_op jit(solution)/shard_map/reduce_scatter | solution.py:161
  105.1 1.7 %add_convert_fusion = bf16[64,1024]{1,0:T(8,128)(2,1)} fusion(f32[64,1024]{1,0:T(8,128)} %reduce-scatter.2.cloned.1.call-done, bf16[64,1024]{1,0:T(8,128)(2,1)S(1)} %gather_fusion.1, pred[64]{0:T(512)(128)(4,1)S(1)} %compare_and_fusion.1), kind=kLoop, calls=%fused_computation.52 | loop fusion | flops 262144 | bytes 524352 | tf_op jit(solution)/shard_map/convert_element_type | solution.py:162
  (30 shorter events, 0.4 us)
Async XLA Ops:
  6.5 37.9 %copy-start.4 = (s32[1,64]{1,0:T(1,128)S(1)}, s32[1,64]{1,0:T(1,128)}, u32[]{:S(2)}) copy-start(s32[1,64]{1,0:T(1,128)} %param.12) | copy-start | bytes 772
  31.0 17.4 %copy-start.2 = (s32[1,64,64]{2,1,0:T(8,128)S(1)}, s32[1,64,64]{2,1,0:T(8,128)}, u32[]{:S(2)}) copy-start(s32[1,64,64]{2,1,0:T(8,128)} %param.13) | copy-start | bytes 49156
  31.0 17.6 %copy-start.3 = (bf16[4096]{0:T(1024)(128)(2,1)S(1)}, bf16[4096]{0:T(1024)(128)(2,1)}, u32[]{:S(2)}) copy-start(bf16[4096]{0:T(1024)(128)(2,1)} %param.16) | copy-start | bytes 24580
  41.0 11.6 %all-to-all-start = ((bf16[8,16,1024]{2,1,0:T(8,128)(2,1)}), bf16[8,16,1024]{2,1,0:T(8,128)(2,1)S(1)}, u32[]{:S(2)}, u32[]{:S(2)}) async-start(bf16[8,16,1024]{2,1,0:T(8,128)(2,1)} %select_select_fusion), calls=%async_computation | async-start | bytes 524288 | tf_op jit(solution)/shard_map/all_to_all | solution.py:110
  44.4 60.8 %reduce-scatter.2.cloned.1.call-start = ((), (), s32[]{:S(2)}) async-start(), calls=%async_computation.2 | async-start | bytes 1310720 | tf_op jit(solution)/shard_map/reduce_scatter | solution.py:161
  63.6 5.7 %copy-start = (bf16[1,2,1024,128]{3,2,1,0:T(8,128)(2,1)S(1)}, bf16[1,2,1024,128]{3,2,1,0:T(8,128)(2,1)}, u32[]{:S(2)}) copy-start(bf16[1,2,1024,128]{3,2,1,0:T(8,128)(2,1)} %param.21) | copy-start | bytes 1572868
  63.6 5.7 %copy-start.1 = (bf16[1,2,1024,128]{3,2,1,0:T(8,128)(2,1)S(1)}, bf16[1,2,1024,128]{3,2,1,0:T(8,128)(2,1)}, u32[]{:S(2)}) copy-start(bf16[1,2,1024,128]{3,2,1,0:T(8,128)(2,1)} %param.20) | copy-start | bytes 1572868
Sparse Core Ops, SparseCore 0:
  80.4 24.6 reduce-scatter.1
where the time goes:
time: 114 us
  blocking collectives  29.6 us (26%)
  waiting for transfers between devices  25.6 us (22%)
  local copies, waits for them, and re-layouts  17.6 us (15%)
  matrix products  16.2 us (14%)
  between operations  14.3 us (13%)
  other arithmetic  6.69 us (6%)
  starting transfers between devices  3.45 us (3%)
    reduce_scatter x1, waiting for transfers between devices, shards(): lax.psum_scatter(partial_out, 'tensor', scatter_dimension=1, tiled=True)  24.9 us
    all_gather x1, blocking collectives, shards(): all_ids = lax.all_gather(tree_ids, 'dp', axis=0, tiled=True).reshape(-1)  22.5 us
    gather x1, local copies, waits for them, and re-layouts, shards(): jnp.take(table, source_offsets.reshape(-1), axis=0)  8.97 us
    all_gather x1, blocking collectives, shards(): lax.all_gather(embedded, 'tensor', axis=1, tiled=True).astype(jnp.float32)  7.17 us
    dot_general x2, local copies, waits for them, and re-layouts, shards(): keys_new = jnp.dot(normed, w_kv[0], preferred_element_type=jnp.float32)  6 us
    dot_general x1, matrix products, shards(): partial_out = jnp.dot(contexts, w_out, preferred_element_type=jnp.float32)  5.94 us
    dot_general x1, matrix products, shards(): queries = jnp.dot(normed, w_query, preferred_element_type=jnp.float32)  5.09 us
    all_to_all x1, starting transfers between devices, shards(): lax.all_to_all(slot_rows, 'dp', split_axis=0, concat_axis=0, tiled=True)  3.41 us
  transfers between devices with their start and end apart: 2, of which 2 were waited for; matrix products, arithmetic and copies ran while one was open for 6% of the time, Pallas kernels for 0%

commit v1 on v0

v1 whole, which is shorter than its diff:
```python
import functools
import math

import jax
import jax.numpy as jnp
from jax import lax
from jax.experimental import pallas as pl
from jax.experimental.pallas import tpu as pltpu
from jax.sharding import PartitionSpec as P

EPS = 1e-05
NEG = -1e30
THETA = 500000.0
MESH = pl.DeviceIdType.MESH
LANES = 128


def layer_kernel(
    n_dp,
    n_t,
    nodes,
    capacity,
    ids_ref,
    anc_ref,
    live_ref,
    cos_ref,
    sin_ref,
    gain_ref,
    table_hbm,
    wq_hbm,
    wkv_hbm,
    wout_hbm,
    kc_hbm,
    vc_hbm,
    out_ref,
    ids_all,
    table_v,
    wq_v,
    wkv_v,
    wout_v,
    kc_v,
    vc_v,
    acc,
    slot_send,
    slot_recv,
    emb_all,
    ctx_v,
    rs1_send,
    rs1_recv,
    rs2_send,
    rs2_recv,
    table_sem,
    w_sem,
    wout_sem,
    ids_ssem,
    ids_rsem,
    row_ssem,
    row_rsem,
    own_sem,
    ag_ssem,
    ag_rsem,
    fw_ssem,
    rs1_ssem,
    rs1_rsem,
    rs2_ssem,
    rs2_rsem,
):
    me = lax.axis_index("dp")
    t = lax.axis_index("tensor")
    chip = t // 2
    parity = t % 2
    partner = t + 1 - 2 * parity
    n_chip = n_t // 2
    vocab_rows, width = table_v.shape
    head_dim = kc_v.shape[-1]
    kv_local = kc_v.shape[0]
    heads = wq_v.shape[1] // head_dim
    groups = heads // kv_local
    slots = n_dp * capacity

    n_tab = table_sem.shape[0]
    tab_step = vocab_rows // n_tab
    table_copies = [
        pltpu.make_async_copy(
            table_hbm.at[pl.ds(i * tab_step, tab_step)],
            table_v.at[pl.ds(i * tab_step, tab_step)],
            table_sem.at[i],
        )
        for i in range(n_tab)
    ]
    for copy in table_copies:
        copy.start()

    barrier = pltpu.get_barrier_semaphore()
    for k in range(1, n_dp):
        pl.semaphore_signal(
            barrier, inc=1, device_id={"dp": lax.rem(me + k, n_dp)}, device_id_type=MESH
        )
    for k in range(1, n_t):
        pl.semaphore_signal(
            barrier, inc=1, device_id={"tensor": lax.rem(t + k, n_t)}, device_id_type=MESH
        )
    pl.semaphore_wait(barrier, n_dp + n_t - 2)

    def dp_copy(src, dst, ssem, rsem, k):
        return pltpu.make_async_remote_copy(
            src_ref=src,
            dst_ref=dst,
            send_sem=ssem,
            recv_sem=rsem,
            device_id={"dp": lax.rem(me + k, n_dp)},
            device_id_type=MESH,
        )

    def t_copy(src, dst, ssem, rsem, target):
        return pltpu.make_async_remote_copy(
            src_ref=src,
            dst_ref=dst,
            send_sem=ssem,
            recv_sem=rsem,
            device_id={"tensor": target},
            device_id_type=MESH,
        )

    ids_copies = [
        dp_copy(ids_ref, ids_all.at[k], ids_ssem.at[k], ids_rsem.at[k], k)
        for k in range(1, n_dp)
    ]
    for copy in ids_copies:
        copy.start()

    sub = lax.broadcasted_iota(jnp.int32, (LANES, LANES), 0)
    lane = lax.broadcasted_iota(jnp.int32, (LANES, LANES), 1)
    earlier = (sub < lane).astype(jnp.float32).astype(jnp.bfloat16)
    slot_index = lax.broadcasted_iota(jnp.int32, (slots, LANES), 0)
    slot_block = slot_index // capacity
    slot_rank = (slot_index - slot_block * capacity).astype(jnp.float32)

    def hits(ids, base):
        mine = (ids >= base) & (ids < base + vocab_rows)
        mine_f = mine.astype(jnp.float32)
        rank = jnp.dot(
            mine_f.astype(jnp.bfloat16), earlier, preferred_element_type=jnp.float32
        )
        return mine & (rank == slot_rank)

    own_ids = jnp.broadcast_to(ids_ref[...], (slots, LANES))
    own_base = lax.rem(me - slot_block + n_dp, n_dp) * vocab_rows
    place = hits(own_ids, own_base).astype(jnp.float32).astype(jnp.bfloat16)

    for copy in ids_copies:
        copy.wait_recv()

    w_copies = [
        pltpu.make_async_copy(wq_hbm, wq_v, w_sem.at[0]),
        pltpu.make_async_copy(wkv_hbm, wkv_v, w_sem.at[1]),
        pltpu.make_async_copy(kc_hbm.at[0], kc_v, w_sem.at[2]),
        pltpu.make_async_copy(vc_hbm.at[0], vc_v, w_sem.at[3]),
    ]
    wout_copies = []
    for k in range(n_chip):
        target_chip = lax.rem(chip + k, n_chip)
        for which in range(2):
            chunk = 2 * target_chip + (parity if which else 1 - parity)
            start = pl.multiple_of(chunk * width, width)
            wout_copies.append(
                pltpu.make_async_copy(
                    wout_hbm.at[:, pl.ds(start, width)],
                    wout_v.at[2 * k + which],
                    wout_sem.at[2 * k + which],
                )
            )
    for copy in w_copies + wout_copies:
        copy.start()

    rows_ids = jnp.concatenate(
        [
            jnp.broadcast_to(ids_ref[...] if k == 0 else ids_all[k], (capacity, LANES))
            for k in range(n_dp)
        ],
        axis=0,
    )
    base = me * vocab_rows
    hit = hits(rows_ids, base)
    offset = (
        jnp.sum(
            jnp.where(hit, (rows_ids - base + 1).astype(jnp.float32), 0.0),
            axis=1,
            keepdims=True,
        )
        - 1.0
    ).astype(jnp.int32)
    for copy in table_copies:
        copy.wait()
    step = min(512, vocab_rows)
    step_lane = lax.broadcasted_iota(jnp.int32, (slots, step), 1)
    acc[...] = jnp.zeros_like(acc)

    def table_step(i, carry):
        first = pl.multiple_of(i * step, step)
        pick = ((step_lane + first) == offset).astype(jnp.float32).astype(jnp.bfloat16)
        acc[...] += jnp.dot(
            pick, table_v[pl.ds(first, step), :], preferred_element_type=jnp.float32
        )
        return carry

    lax.fori_loop(0, vocab_rows // step, table_step, 0)
    for k in range(n_dp):
        slot_send[k] = acc[k * capacity : (k + 1) * capacity, :].astype(jnp.bfloat16)
    row_copies = []
    for k in range(1, n_dp):
        back = n_dp - k
        row_copies.append(
            dp_copy(slot_send.at[k], slot_recv.at[back], row_ssem.at[k], row_rsem.at[back], back)
        )
    for copy in row_copies:
        copy.start()
    slot_recv[0] = slot_send[0]
    for k in range(1, n_dp):
        dp_copy(slot_send.at[k], slot_recv.at[k], row_ssem.at[k], row_rsem.at[k], k).wait_recv()
    arrived = slot_recv[...].reshape(slots, width)
    embedded = lax.dot_general(
        place, arrived, (((0,), (0,)), ((), ())), preferred_element_type=jnp.float32
    )[:nodes]
    emb_all[t] = embedded.astype(jnp.bfloat16)

    ag_copies = [
        t_copy(emb_all.at[t], emb_all.at[t], ag_ssem.at[k], ag_rsem.at[t],
               lax.rem(t + 2 * k, n_t) if k else partner)
        for k in range(n_chip)
    ]
    for copy in ag_copies[1:] + ag_copies[:1]:
        copy.start()

    def ag_wait(origin):
        t_copy(emb_all.at[origin], emb_all.at[origin], ag_ssem.at[0], ag_rsem.at[origin],
               partner).wait_recv()

    fw_copies = []
    for k in range(1, n_chip):
        origin = lax.rem(t - 2 * k + n_t, n_t)
        ag_wait(origin)
        copy = t_copy(emb_all.at[origin], emb_all.at[origin], fw_ssem.at[k], ag_rsem.at[origin],
                      partner)
        copy.start()
        fw_copies.append(copy)
    ag_wait(partner)
    for k in range(1, n_chip):
        ag_wait(lax.rem(partner - 2 * k + n_t, n_t))

    squares = jnp.zeros((nodes, 1), jnp.float32)
    for j in range(n_t):
        features = emb_all[j].astype(jnp.float32)
        squares = squares + jnp.sum(features * features, axis=1, keepdims=True)
    inv_rms = lax.rsqrt(squares / (n_t * width) + EPS)
    for copy in w_copies:
        copy.wait()
    queries = jnp.zeros((nodes, wq_v.shape[1]), jnp.float32)
    keys_raw = jnp.zeros((nodes, wkv_v.shape[2]), jnp.float32)
    values_raw = jnp.zeros((nodes, wkv_v.shape[2]), jnp.float32)
    for j in range(n_t):
        span = slice(j * width, (j + 1) * width)
        gain = gain_ref[:, span].astype(jnp.float32)
        normed = (emb_all[j].astype(jnp.float32) * inv_rms * gain).astype(jnp.bfloat16)
        queries = queries + jnp.dot(normed, wq_v[span, :], preferred_element_type=jnp.float32)
        keys_raw = keys_raw + jnp.dot(normed, wkv_v[0, span, :], preferred_element_type=jnp.float32)
        values_raw = values_raw + jnp.dot(
            normed, wkv_v[1, span, :], preferred_element_type=jnp.float32
        )
    values_new = values_raw.astype(jnp.bfloat16)
    cosine = cos_ref[...]
    sine = sin_ref[...]

    def rotary(values):
        return (values * cosine + pltpu.roll(values, head_dim // 2, 1) * sine).astype(jnp.bfloat16)

    scale = head_dim ** (-0.5)
    live = live_ref[...] > 0
    tree = jnp.concatenate([anc_ref[0]] * groups, axis=0) > 0
    contract = (((1,), (1,)), ((), ()))
    for kv in range(kv_local):
        cols = slice(kv * head_dim, (kv + 1) * head_dim)
        query = jnp.concatenate(
            [
                rotary(queries[:, h * head_dim : (h + 1) * head_dim])
                for h in range(kv * groups, (kv + 1) * groups)
            ],
            axis=0,
        )
        key_tree = rotary(keys_raw[:, cols])
        cache_scores = (
            lax.dot_general(query, kc_v[kv], contract, preferred_element_type=jnp.float32) * scale
        )
        cache_scores = jnp.where(live, cache_scores, NEG)
        tree_scores = (
            lax.dot_general(query, key_tree, contract, preferred_element_type=jnp.float32) * scale
        )
        tree_scores = jnp.where(tree, tree_scores, NEG)
        top = jnp.maximum(
            jnp.max(cache_scores, axis=1, keepdims=True),
            jnp.max(tree_scores, axis=1, keepdims=True),
        )
        cache_exp = jnp.exp(cache_scores - top)
        tree_exp = jnp.exp(tree_scores - top)
        denominator = jnp.sum(cache_exp, axis=1, keepdims=True) + jnp.sum(
            tree_exp, axis=1, keepdims=True
        )
        weighted = jnp.dot(
            tree_exp.astype(jnp.bfloat16), values_new[:, cols], preferred_element_type=jnp.float32
        ) + jnp.dot(cache_exp.astype(jnp.bfloat16), vc_v[kv], preferred_element_type=jnp.float32)
        context = (weighted / denominator).astype(jnp.bfloat16)
        for g in range(groups):
            h = kv * groups + g
            ctx_v[:, h * head_dim : (h + 1) * head_dim] = context[g * nodes : (g + 1) * nodes]

    for copy in wout_copies:
        copy.wait()
    contexts = ctx_v[...]
    order = list(range(1, n_chip)) + [0]
    rs1_copies = {}
    for k in order:
        part = jnp.dot(contexts, wout_v[2 * k], preferred_element_type=jnp.float32)
        rs1_send[k] = part.astype(jnp.bfloat16)
        rs1_copies[k] = t_copy(
            rs1_send.at[k], rs1_recv.at[k], rs1_ssem.at[k], rs1_rsem.at[k], partner
        )
        rs1_copies[k].start()
    rs2_copies = []
    total = None
    for k in order:
        part = jnp.dot(contexts, wout_v[2 * k + 1], preferred_element_type=jnp.float32)
        rs1_copies[k].wait_recv()
        both = part + rs1_recv[k].astype(jnp.float32)
        if k:
            rs2_send[k] = both.astype(jnp.bfloat16)
            copy = t_copy(
                rs2_send.at[k], rs2_recv.at[k], rs2_ssem.at[k], rs2_rsem.at[k],
                lax.rem(t + 2 * k, n_t),
            )
            copy.start()
            rs2_copies.append(copy)
        else:
            total = both
    total = total + emb_all[t].astype(jnp.float32)
    for k, copy in enumerate(rs2_copies):
        copy.wait_recv()
        total = total + rs2_recv[k + 1].astype(jnp.float32)
    out_ref[...] = total.astype(jnp.bfloat16)
    for copy in (
        ids_copies + row_copies + ag_copies + fw_copies + list(rs1_copies.values()) + rs2_copies
    ):
        copy.wait_send()


def shards(tree_ids, ancestors, lengths, table, gain, w_query, w_kv, w_out, key_cache, value_cache):
    n_dp = lax.axis_size("dp")
    n_t = lax.axis_size("tensor")
    n_chip = n_t // 2
    row_count, nodes = tree_ids.shape
    vocab_rows, width = table.shape
    head_dim = key_cache.shape[3]
    context = key_cache.shape[2]
    kv_local = key_cache.shape[1]
    capacity = 2 * ((row_count * nodes + n_dp - 1) // n_dp)
    capacity = 16 * ((capacity + 15) // 16)
    ids = jnp.pad(tree_ids, ((0, 0), (0, LANES - nodes)), constant_values=-1)
    half_dim = head_dim // 2
    inverse = jnp.exp(
        jnp.arange(half_dim, dtype=jnp.float32) * (-2.0 * math.log(THETA) / head_dim)
    )
    positions = (lengths[:, None] + jnp.sum(ancestors, axis=2) - 1).reshape(-1)
    angles = positions.astype(jnp.float32)[:, None] * inverse[None, :]
    cosine = jnp.cos(angles)
    sine = jnp.sin(angles)
    cosine = jnp.concatenate([cosine, cosine], axis=1)
    sine = jnp.concatenate([-sine, sine], axis=1)
    live = (jnp.arange(context, dtype=jnp.int32)[None, :] < lengths[:, None]).astype(jnp.int32)
    bf16, f32 = jnp.bfloat16, jnp.float32
    n_tab = 4
    sems = pltpu.SemaphoreType.DMA
    vmem = pl.BlockSpec(memory_space=pltpu.VMEM)
    hbm = pl.BlockSpec(memory_space=pl.ANY)
    return pl.pallas_call(
        functools.partial(layer_kernel, n_dp, n_t, nodes, capacity),
        out_shape=jax.ShapeDtypeStruct((nodes, width), bf16),
        in_specs=[vmem] * 6 + [hbm] * 6,
        out_specs=vmem,
        scratch_shapes=[
            pltpu.VMEM((n_dp, 1, LANES), jnp.int32),
            pltpu.VMEM(table.shape, bf16),
            pltpu.VMEM(w_query.shape, bf16),
            pltpu.VMEM(w_kv.shape, bf16),
            pltpu.VMEM((n_t, w_out.shape[0], width), bf16),
            pltpu.VMEM(key_cache.shape[1:], bf16),
            pltpu.VMEM(value_cache.shape[1:], bf16),
            pltpu.VMEM((n_dp * capacity, width), f32),
            pltpu.VMEM((n_dp, capacity, width), bf16),
            pltpu.VMEM((n_dp, capacity, width), bf16),
            pltpu.VMEM((n_t, nodes, width), bf16),
            pltpu.VMEM((nodes, w_query.shape[1]), bf16),
            pltpu.VMEM((n_chip, nodes, width), bf16),
            pltpu.VMEM((n_chip, nodes, width), bf16),
            pltpu.VMEM((n_chip, nodes, width), bf16),
            pltpu.VMEM((n_chip, nodes, width), bf16),
            sems((n_tab,)),
            sems((4,)),
            sems((n_t,)),
            sems((n_dp,)),
            sems((n_dp,)),
            sems((n_dp,)),
            sems((n_dp,)),
            sems((1,)),
            sems((n_chip,)),
            sems((n_t,)),
            sems((n_chip,)),
            sems((n_chip,)),
            sems((n_chip,)),
            sems((n_chip,)),
            sems((n_chip,)),
        ],
        compiler_params=pltpu.CompilerParams(
            collective_id=0, has_side_effects=True, vmem_limit_bytes=62 * 1024 * 1024
        ),
    )(
        ids,
        ancestors,
        live,
        cosine,
        sine,
        gain.reshape(1, -1),
        table,
        w_query,
        w_kv,
        w_out,
        key_cache,
        value_cache,
    )


def solution(mesh):
    in_specs = (
        P("dp", None),
        P("dp", None, None),
        P("dp"),
        P("dp", "tensor"),
        P(),
        P(None, "tensor"),
        P(None, None, "tensor"),
        P("tensor", None),
        P("dp", "tensor", None, None),
        P("dp", "tensor", None, None),
    )
    out_specs = P("dp", "tensor")
    return jax.shard_map(shards, mesh=mesh, in_specs=in_specs, out_specs=out_specs, check_vma=False)
```

time: 114 us -> 47.6 us (0.42)
  Pallas kernels: 0 us -> 40.1 us
  blocking collectives: 29.6 us -> 0 us
  waiting for transfers between devices: 25.6 us -> 0 us
  matrix products: 16.2 us -> 0 us
  between operations: 14.3 us -> 0.68 us
  local copies, waits for them, and re-layouts: 17.6 us -> 4.11 us
  other arithmetic: 6.69 us -> 2.38 us
  starting transfers between devices: 3.45 us -> 0 us
    pallas_call x0 -> x1, Pallas kernels: none -> 40.1 us  [shards(): pl.pallas_call(functools.partial(layer_kernel, n_dp, n_t, nodes, capacity...]
    all_gather x2 -> x0, blocking collectives: 29.6 us -> none  [the longest x1 22.5 us: shards(): all_ids = lax.all_gather(tree_ids, 'dp', axis=0, tiled=True).reshape(-1)]
    reduce_scatter x1 -> x0, waiting for transfers between devices: 24.9 us -> none  [shards(): lax.psum_scatter(partial_out, 'tensor', scatter_dimension=1, tiled=True)]
    dot_general x12 -> x0, matrix products: 16.2 us -> none  [the longest x1 5.94 us: shards(): partial_out = jnp.dot(contexts, w_out, preferred_element_type=jnp.float32)]
    gather x5 -> x0, local copies, waits for them, and re-layouts: 10.8 us -> none  [the longest x1 8.97 us: shards(): jnp.take(table, source_offsets.reshape(-1), axis=0)]
    dot_general x2 -> x0, local copies, waits for them, and re-layouts: 6 us -> none  [shards(): keys_new = jnp.dot(normed, w_kv[0], preferred_element_type=jnp.float32)]
    all_to_all x1 -> x0, starting transfers between devices: 3.41 us -> none  [shards(): lax.all_to_all(slot_rows, 'dp', split_axis=0, concat_axis=0, tiled=True)]
    unnamed x12 -> x1, local copies, waits for them, and re-layouts: 0.15 us -> 1.57 us
  transfers between devices with their start and end apart: 2 -> 0, of which waited for: 2 -> 0; matrix products, arithmetic and copies ran while one was open for 6% -> 0% of each run, Pallas kernels for 0% -> 0%
where the time goes in v1:
time: 47.6 us; the launch traced here: 47.3 us
  Pallas kernels  40.1 us (84%)
  local copies, waits for them, and re-layouts  4.11 us (9%)
  other arithmetic  2.38 us (5%)
  between operations  0.68 us (1%)
    pallas_call x1, Pallas kernels, shards(): pl.pallas_call(functools.partial(layer_kernel, n_dp, n_t, nodes, capacity...  40.1 us
    unnamed x1, local copies, waits for them, and re-layouts  1.57 us
    reshape x1, local copies, waits for them, and re-layouts, shards(): gain.reshape(1, -1)  1.3 us
    pad x1, local copies, waits for them, and re-layouts, shards(): ids = jnp.pad(tree_ids, ((0, 0), (0, LANES - nodes)), constant_values=-1)  1.23 us

profile of v1, /device:TPU:0, one launch (start us, length us, event | category | flops | bytes accessed | tf_op | source)
XLA Modules:
  0.0 47.3 jit_solution(11333902981247057965)
XLA Ops:
  0.7 1.2 %pad.4.ids_ref = s32[1,128]{1,0:T(1,128)} pad(s32[1,64]{1,0:T(1,128)} %param.10, s32[]{:T(128)} %constant.3.clone.1), padding=0_0x0_64 | pad | bytes 772 | tf_op jit(solution)/shard_map/jit(_pad)/pad | solution.py:366
  1.9 0.9 %reduce_sum.9 = s32[64]{0:T(128)S(1)} reduce(s32[1,64,64]{2,1,0:T(8,128)} %anc_ref.1, s32[]{:T(128)} %constant.1.clone.1), dimensions={0,2}, to_apply=%region_0.1 | reduce | flops 4032 | bytes 16644 | tf_op jit(solution)/shard_map/reduce_sum | solution.py:371
  2.8 0.6 %compare_convert_fusion.live_ref = s32[1,1024]{1,0:T(1,128)} fusion(s32[]{:T(128)} %bitcast.1), kind=kLoop, calls=%fused_computation.4 | loop fusion | flops 2048 | bytes 4100 | tf_op jit(solution)/shard_map/convert_element_type | solution.py:377
  3.4 1.3 %reshape.36.gain_ref = bf16[1,4096]{1,0:T(2,128)(2,1)} reshape(bf16[4096]{0:T(1024)(128)(2,1)} %param.14) | data formatting | bytes 16384 | tf_op jit(solution)/shard_map/reshape | solution.py:430
  4.7 0.2 fusion
  4.9 0.7 %pad_maximum_fusion = (f32[64,128]{1,0:T(8,128)}, f32[64,128]{1,0:T(8,128)}) fusion(f32[64,64]{1,0:T(8,128)S(1)} %get-tuple-element.7, f32[64,64]{1,0:T(8,128)S(1)} %get-tuple-element.6, f32[64,64]{1,0:T(8,128)S(1)} %get-tuple-element.5), kind=kLoop, calls=%fused_computation.2 | loop fusion | flops 16384 | bytes 114688 | tf_op jit(solution)/shard_map/concatenate | solution.py:375
  5.6 40.1 %shard_map.100 = bf16[64,1024]{1,0:T(8,128)(2,1)} custom-call(s32[1,128]{1,0:T(1,128)} %pad.4.ids_ref, s32[1,64,64]{2,1,0:T(8,128)} %anc_ref.1, s32[1,1024]{1,0:T(1,128)} %compare_convert_fusion.live_ref, f32[64,128]{1,0:T(8,128)} %get-tuple-element.8.cos_ref, f32[64,128]{1,0:T(8,128)} %get-tuple-element.9.sin_ref, bf16[1,4096]{1,0:T(2,128)(2,1)} %reshape.36.gain_ref, ...), custom_call_target="tpu_custom_call" | custom-call | tf_op jit(solution)/shard_map/pallas_call | solution.py:383
  45.7 1.6 %copy.13 = bf16[64,1024]{1,0:T(8,128)(2,1)} copy(bf16[64,1024]{1,0:T(8,128)(2,1)} %shard_map.100) | data formatting | bytes 262144
  (2 shorter events, 0.0 us)

commit v2 on v1

--- a/solution.py
+++ b/solution.py
@@ -12,7 +12,6 @@
 NEG = -1e30
 THETA = 500000.0
 MESH = pl.DeviceIdType.MESH
-LANES = 128
 
 
 def layer_kernel(
@@ -22,9 +21,7 @@
     capacity,
     ids_ref,
     anc_ref,
-    live_ref,
-    cos_ref,
-    sin_ref,
+    len_ref,
     gain_ref,
     table_hbm,
     wq_hbm,
@@ -34,6 +31,8 @@
     vc_hbm,
     out_ref,
     ids_all,
+    cos_v,
+    sin_v,
     table_v,
     wq_v,
     wkv_v,
@@ -78,6 +77,15 @@
     groups = heads // kv_local
     slots = n_dp * capacity
 
+    barrier = pltpu.get_barrier_semaphore()
+    for k in range(1, n_dp):
+        pl.semaphore_signal(
+            barrier, inc=1, device_id={"dp": lax.rem(me + k, n_dp)}, device_id_type=MESH
+        )
+    for k in range(1, n_t):
+        pl.semaphore_signal(
+            barrier, inc=1, device_id={"tensor": lax.rem(t + k, n_t)}, device_id_type=MESH
+        )
     n_tab = table_sem.shape[0]
     tab_step = vocab_rows // n_tab
     table_copies = [
@@ -91,15 +99,6 @@
     for copy in table_copies:
         copy.start()
 
-    barrier = pltpu.get_barrier_semaphore()
-    for k in range(1, n_dp):
-        pl.semaphore_signal(
-            barrier, inc=1, device_id={"dp": lax.rem(me + k, n_dp)}, device_id_type=MESH
-        )
-    for k in range(1, n_t):
-        pl.semaphore_signal(
-            barrier, inc=1, device_id={"tensor": lax.rem(t + k, n_t)}, device_id_type=MESH
-        )
     pl.semaphore_wait(barrier, n_dp + n_t - 2)
 
     def dp_copy(src, dst, ssem, rsem, k):
@@ -129,10 +128,10 @@
     for copy in ids_copies:
         copy.start()
 
-    sub = lax.broadcasted_iota(jnp.int32, (LANES, LANES), 0)
-    lane = lax.broadcasted_iota(jnp.int32, (LANES, LANES), 1)
+    sub = lax.broadcasted_iota(jnp.int32, (nodes, nodes), 0)
+    lane = lax.broadcasted_iota(jnp.int32, (nodes, nodes), 1)
     earlier = (sub < lane).astype(jnp.float32).astype(jnp.bfloat16)
-    slot_index = lax.broadcasted_iota(jnp.int32, (slots, LANES), 0)
+    slot_index = lax.broadcasted_iota(jnp.int32, (slots, nodes), 0)
     slot_block = slot_index // capacity
     slot_rank = (slot_index - slot_block * capacity).astype(jnp.float32)
 
@@ -144,9 +143,20 @@
         )
         return mine & (rank == slot_rank)
 
-    own_ids = jnp.broadcast_to(ids_ref[...], (slots, LANES))
+    own_ids = jnp.broadcast_to(ids_ref[...], (slots, nodes))
     own_base = lax.rem(me - slot_block + n_dp, n_dp) * vocab_rows
     place = hits(own_ids, own_base).astype(jnp.float32).astype(jnp.bfloat16)
+
+    depth = jnp.sum(anc_ref[0].astype(jnp.float32), axis=1, keepdims=True)
+    positions = depth + (len_ref[0] - 1).astype(jnp.float32)
+    half_dim = head_dim // 2
+    lanes = lax.broadcasted_iota(jnp.int32, (1, head_dim), 1)
+    freq_index = jnp.where(lanes < half_dim, lanes, lanes - half_dim).astype(jnp.float32)
+    angles = positions * jnp.exp(freq_index * (-2.0 * math.log(THETA) / head_dim))
+    cosine = jnp.cos(angles)
+    sine = jnp.where(lanes < half_dim, -jnp.sin(angles), jnp.sin(angles))
+    cos_v[...] = cosine
+    sin_v[...] = sine
 
     for copy in ids_copies:
         copy.wait_recv()
@@ -175,7 +185,7 @@
 
     rows_ids = jnp.concatenate(
         [
-            jnp.broadcast_to(ids_ref[...] if k == 0 else ids_all[k], (capacity, LANES))
+            jnp.broadcast_to(ids_ref[...] if k == 0 else ids_all[k], (capacity, nodes))
             for k in range(n_dp)
         ],
         axis=0,
@@ -260,7 +270,7 @@
     values_raw = jnp.zeros((nodes, wkv_v.shape[2]), jnp.float32)
     for j in range(n_t):
         span = slice(j * width, (j + 1) * width)
-        gain = gain_ref[:, span].astype(jnp.float32)
+        gain = gain_ref[span].astype(jnp.float32)[None, :]
         normed = (emb_all[j].astype(jnp.float32) * inv_rms * gain).astype(jnp.bfloat16)
         queries = queries + jnp.dot(normed, wq_v[span, :], preferred_element_type=jnp.float32)
         keys_raw = keys_raw + jnp.dot(normed, wkv_v[0, span, :], preferred_element_type=jnp.float32)
@@ -268,14 +278,14 @@
             normed, wkv_v[1, span, :], preferred_element_type=jnp.float32
         )
     values_new = values_raw.astype(jnp.bfloat16)
-    cosine = cos_ref[...]
-    sine = sin_ref[...]
+    cosine = cos_v[...]
+    sine = sin_v[...]
 
     def rotary(values):
         return (values * cosine + pltpu.roll(values, head_dim // 2, 1) * sine).astype(jnp.bfloat16)
 
     scale = head_dim ** (-0.5)
-    live = live_ref[...] > 0
+    live = lax.broadcasted_iota(jnp.int32, (1, kc_v.shape[1]), 1) < len_ref[0]
     tree = jnp.concatenate([anc_ref[0]] * groups, axis=0) > 0
     contract = (((1,), (1,)), ((), ()))
     for kv in range(kv_local):
@@ -345,7 +355,7 @@
     for k, copy in enumerate(rs2_copies):
         copy.wait_recv()
         total = total + rs2_recv[k + 1].astype(jnp.float32)
-    out_ref[...] = total.astype(jnp.bfloat16)
+    out_ref[...] = total
     for copy in (
         ids_copies + row_copies + ag_copies + fw_copies + list(rs1_copies.values()) + rs2_copies
     ):
@@ -359,22 +369,8 @@
     row_count, nodes = tree_ids.shape
     vocab_rows, width = table.shape
     head_dim = key_cache.shape[3]
-    context = key_cache.shape[2]
-    kv_local = key_cache.shape[1]
     capacity = 2 * ((row_count * nodes + n_dp - 1) // n_dp)
     capacity = 16 * ((capacity + 15) // 16)
-    ids = jnp.pad(tree_ids, ((0, 0), (0, LANES - nodes)), constant_values=-1)
-    half_dim = head_dim // 2
-    inverse = jnp.exp(
-        jnp.arange(half_dim, dtype=jnp.float32) * (-2.0 * math.log(THETA) / head_dim)
-    )
-    positions = (lengths[:, None] + jnp.sum(ancestors, axis=2) - 1).reshape(-1)
-    angles = positions.astype(jnp.float32)[:, None] * inverse[None, :]
-    cosine = jnp.cos(angles)
-    sine = jnp.sin(angles)
-    cosine = jnp.concatenate([cosine, cosine], axis=1)
-    sine = jnp.concatenate([-sine, sine], axis=1)
-    live = (jnp.arange(context, dtype=jnp.int32)[None, :] < lengths[:, None]).astype(jnp.int32)
     bf16, f32 = jnp.bfloat16, jnp.float32
     n_tab = 4
     sems = pltpu.SemaphoreType.DMA
@@ -382,11 +378,13 @@
     hbm = pl.BlockSpec(memory_space=pl.ANY)
     return pl.pallas_call(
         functools.partial(layer_kernel, n_dp, n_t, nodes, capacity),
-        out_shape=jax.ShapeDtypeStruct((nodes, width), bf16),
-        in_specs=[vmem] * 6 + [hbm] * 6,
+        out_shape=jax.ShapeDtypeStruct((nodes, width), f32),
+        in_specs=[vmem, vmem, pl.BlockSpec(memory_space=pltpu.SMEM), vmem] + [hbm] * 6,
         out_specs=vmem,
         scratch_shapes=[
-            pltpu.VMEM((n_dp, 1, LANES), jnp.int32),
+            pltpu.VMEM((n_dp, 1, nodes), jnp.int32),
+            pltpu.VMEM((nodes, head_dim), f32),
+            pltpu.VMEM((nodes, head_dim), f32),
             pltpu.VMEM(table.shape, bf16),
             pltpu.VMEM(w_query.shape, bf16),
             pltpu.VMEM(w_kv.shape, bf16),
@@ -422,19 +420,17 @@
             collective_id=0, has_side_effects=True, vmem_limit_bytes=62 * 1024 * 1024
         ),
     )(
-        ids,
+        tree_ids,
         ancestors,
-        live,
-        cosine,
-        sine,
-        gain.reshape(1, -1),
+        lengths,
+        gain,
         table,
         w_query,
         w_kv,
         w_out,
         key_cache,
         value_cache,
-    )
+    ).astype(bf16)
 
 
 def solution(mesh):

time: 47.6 us -> 42.6 us (0.89)
  local copies, waits for them, and re-layouts: 4.11 us -> 0 us
  other arithmetic: 2.38 us -> 1.62 us
    unnamed x1 -> x0, local copies, waits for them, and re-layouts: 1.57 us -> none
    reshape x1 -> x0, local copies, waits for them, and re-layouts: 1.3 us -> none  [shards(): gain.reshape(1, -1)]
    pad x1 -> x0, local copies, waits for them, and re-layouts: 1.23 us -> none  [shards(): ids = jnp.pad(tree_ids, ((0, 0), (0, LANES - nodes)), constant_values=-1)]
    convert_element_type x2 -> x1, other arithmetic: 0.61 us -> 1.62 us  [shards(): return pl.pallas_call(functools.partial(layer_kernel, n_dp, n_t, nodes, c...]
    reduce_sum x1 -> x0, other arithmetic: 0.86 us -> none  [shards(): positions = (lengths[:, None] + jnp.sum(ancestors, axis=2) - 1).reshape(-1)]
    concatenate x1 -> x0, other arithmetic: 0.71 us -> none  [shards(): cosine = jnp.concatenate([cosine, cosine], axis=1)]
where the time goes in v2:
time: 42.6 us; the launch traced here: 42.4 us
  Pallas kernels  40.1 us (94%)
  other arithmetic  1.62 us (4%)
  between operations  0.66 us (2%)
    pallas_call x1, Pallas kernels, shards(): pl.pallas_call(functools.partial(layer_kernel, n_dp, n_t, nodes, capacity...  40.1 us
    convert_element_type x1, other arithmetic, shards(): return pl.pallas_call(functools.partial(layer_kernel, n_dp, n_t, nodes, c...  1.62 us

profile of v2, /device:TPU:0, one launch (start us, length us, event | category | flops | bytes accessed | tf_op | source)
XLA Modules:
  0.0 42.4 jit_solution(2210345091634903027)
XLA Ops:
  0.7 40.1 %shard_map.100 = f32[64,1024]{1,0:T(8,128)} custom-call(s32[1,64]{1,0:T(1,128)} %ids_ref.1, s32[1,64,64]{2,1,0:T(8,128)} %anc_ref.1, s32[1]{0:T(128)S(6)} %copy.11.len_ref, bf16[4096]{0:T(1024)(128)(2,1)} %gain_ref.1, bf16[8192,1024]{1,0:T(8,128)(2,1)} %table_hbm.1, bf16[4096,1024]{1,0:T(8,128)(2,1)} %wq_hbm.1, bf16[2,4096,256]{2,1,0:T(8,128)(2,1)} %wkv_hbm.1, ...), custom_call_target="tpu_custom_call" | custom-call | tf_op jit(solution)/shard_map/pallas_call | solution.py:379
  40.8 1.6 %convert_element_type.3 = bf16[64,1024]{1,0:T(8,128)(2,1)} convert(f32[64,1024]{1,0:T(8,128)} %shard_map.100) | non-fusion elementwise | flops 65536 | bytes 393216 | tf_op jit(solution)/shard_map/convert_element_type | solution.py:433

commit v3 on v2

--- a/solution.py
+++ b/solution.py
@@ -39,7 +39,7 @@
     wout_v,
     kc_v,
     vc_v,
-    acc,
+    pick_v,
     slot_send,
     slot_recv,
     emb_all,
@@ -55,7 +55,6 @@
     ids_rsem,
     row_ssem,
     row_rsem,
-    own_sem,
     ag_ssem,
     ag_rsem,
     fw_ssem,
@@ -76,6 +75,8 @@
     heads = wq_v.shape[1] // head_dim
     groups = heads // kv_local
     slots = n_dp * capacity
+    n_part = emb_all.shape[0]
+    part_width = width // n_part
 
     barrier = pltpu.get_barrier_semaphore()
     for k in range(1, n_dp):
@@ -200,68 +201,86 @@
         )
         - 1.0
     ).astype(jnp.int32)
+    step = min(512, vocab_rows)
+    step_lane = lax.broadcasted_iota(jnp.int32, (slots, step), 1)
+    for i in range(vocab_rows // step):
+        pick_v[i] = ((step_lane + i * step) == offset).astype(jnp.float32).astype(jnp.bfloat16)
     for copy in table_copies:
         copy.wait()
-    step = min(512, vocab_rows)
-    step_lane = lax.broadcasted_iota(jnp.int32, (slots, step), 1)
-    acc[...] = jnp.zeros_like(acc)
-
-    def table_step(i, carry):
-        first = pl.multiple_of(i * step, step)
-        pick = ((step_lane + first) == offset).astype(jnp.float32).astype(jnp.bfloat16)
-        acc[...] += jnp.dot(
-            pick, table_v[pl.ds(first, step), :], preferred_element_type=jnp.float32
-        )
-        return carry
-
-    lax.fori_loop(0, vocab_rows // step, table_step, 0)
-    for k in range(n_dp):
-        slot_send[k] = acc[k * capacity : (k + 1) * capacity, :].astype(jnp.bfloat16)
+
     row_copies = []
-    for k in range(1, n_dp):
-        back = n_dp - k
-        row_copies.append(
-            dp_copy(slot_send.at[k], slot_recv.at[back], row_ssem.at[k], row_rsem.at[back], back)
-        )
-    for copy in row_copies:
-        copy.start()
-    slot_recv[0] = slot_send[0]
-    for k in range(1, n_dp):
-        dp_copy(slot_send.at[k], slot_recv.at[k], row_ssem.at[k], row_rsem.at[k], k).wait_recv()
-    arrived = slot_recv[...].reshape(slots, width)
-    embedded = lax.dot_general(
-        place, arrived, (((0,), (0,)), ((), ())), preferred_element_type=jnp.float32
-    )[:nodes]
-    emb_all[t] = embedded.astype(jnp.bfloat16)
-
-    ag_copies = [
-        t_copy(emb_all.at[t], emb_all.at[t], ag_ssem.at[k], ag_rsem.at[t],
-               lax.rem(t + 2 * k, n_t) if k else partner)
-        for k in range(n_chip)
-    ]
-    for copy in ag_copies[1:] + ag_copies[:1]:
-        copy.start()
-
-    def ag_wait(origin):
-        t_copy(emb_all.at[origin], emb_all.at[origin], ag_ssem.at[0], ag_rsem.at[origin],
-               partner).wait_recv()
-
+    for q in range(n_part):
+
+        def table_step(i, total, q=q):
+            first = pl.multiple_of(i * step, step)
+            return total + jnp.dot(
+                pick_v[i],
+                table_v[pl.ds(first, step), q * part_width : (q + 1) * part_width],
+                preferred_element_type=jnp.float32,
+            )
+
+        picked = lax.fori_loop(
+            0, vocab_rows // step, table_step, jnp.zeros((slots, part_width), jnp.float32)
+        ).astype(jnp.bfloat16)
+        for k in range(n_dp):
+            slot_send[q, k] = picked[k * capacity : (k + 1) * capacity, :]
+        for k in range(1, n_dp):
+            back = n_dp - k
+            copy = dp_copy(
+                slot_send.at[q, k],
+                slot_recv.at[q, back],
+                row_ssem.at[q, k],
+                row_rsem.at[q, back],
+                back,
+            )
+            copy.start()
+            row_copies.append(copy)
+        slot_recv[q, 0] = slot_send[q, 0]
+
+    def ag_copy(q, origin, ssem, target):
+        return t_copy(
+            emb_all.at[q, origin], emb_all.at[q, origin], ssem, ag_rsem.at[q, origin], target
+        )
+
+    ag_copies = []
     fw_copies = []
-    for k in range(1, n_chip):
-        origin = lax.rem(t - 2 * k + n_t, n_t)
-        ag_wait(origin)
-        copy = t_copy(emb_all.at[origin], emb_all.at[origin], fw_ssem.at[k], ag_rsem.at[origin],
-                      partner)
-        copy.start()
-        fw_copies.append(copy)
-    ag_wait(partner)
-    for k in range(1, n_chip):
-        ag_wait(lax.rem(partner - 2 * k + n_t, n_t))
+
+    def forward(q):
+        for k in range(1, n_chip):
+            origin = lax.rem(t - 2 * k + n_t, n_t)
+            copy = ag_copy(q, origin, fw_ssem.at[q, k], partner)
+            copy.wait_recv()
+            copy.start()
+            fw_copies.append(copy)
+
+    for q in range(n_part):
+        for k in range(1, n_dp):
+            dp_copy(
+                slot_send.at[q, k], slot_recv.at[q, k], row_ssem.at[q, k], row_rsem.at[q, k], k
+            ).wait_recv()
+        arrived = slot_recv[q].reshape(slots, part_width)
+        embedded = lax.dot_general(
+            place, arrived, (((0,), (0,)), ((), ())), preferred_element_type=jnp.float32
+        )
+        emb_all[q, t] = embedded.astype(jnp.bfloat16)
+        for k in list(range(1, n_chip)) + [0]:
+            copy = ag_copy(q, t, ag_ssem.at[q, k], lax.rem(t + 2 * k, n_t) if k else partner)
+            copy.start()
+            ag_copies.append(copy)
+        if q:
+            forward(q - 1)
+    forward(n_part - 1)
+    for q in range(n_part):
+        ag_copy(q, partner, ag_ssem.at[q, 0], partner).wait_recv()
+        for k in range(1, n_chip):
+            origin = lax.rem(partner - 2 * k + n_t, n_t)
+            ag_copy(q, origin, ag_ssem.at[q, 0], partner).wait_recv()
 
     squares = jnp.zeros((nodes, 1), jnp.float32)
     for j in range(n_t):
-        features = emb_all[j].astype(jnp.float32)
-        squares = squares + jnp.sum(features * features, axis=1, keepdims=True)
+        for q in range(n_part):
+            features = emb_all[q, j].astype(jnp.float32)
+            squares = squares + jnp.sum(features * features, axis=1, keepdims=True)
     inv_rms = lax.rsqrt(squares / (n_t * width) + EPS)
     for copy in w_copies:
         copy.wait()
@@ -271,7 +290,8 @@
     for j in range(n_t):
         span = slice(j * width, (j + 1) * width)
         gain = gain_ref[span].astype(jnp.float32)[None, :]
-        normed = (emb_all[j].astype(jnp.float32) * inv_rms * gain).astype(jnp.bfloat16)
+        features = jnp.concatenate([emb_all[q, j] for q in range(n_part)], axis=1)
+        normed = (features.astype(jnp.float32) * inv_rms * gain).astype(jnp.bfloat16)
         queries = queries + jnp.dot(normed, wq_v[span, :], preferred_element_type=jnp.float32)
         keys_raw = keys_raw + jnp.dot(normed, wkv_v[0, span, :], preferred_element_type=jnp.float32)
         values_raw = values_raw + jnp.dot(
@@ -351,7 +371,9 @@
             rs2_copies.append(copy)
         else:
             total = both
-    total = total + emb_all[t].astype(jnp.float32)
+    total = total + jnp.concatenate(
+        [emb_all[q, t].astype(jnp.float32) for q in range(n_part)], axis=1
+    )
     for k, copy in enumerate(rs2_copies):
         copy.wait_recv()
         total = total + rs2_recv[k + 1].astype(jnp.float32)
@@ -373,6 +395,8 @@
     capacity = 16 * ((capacity + 15) // 16)
     bf16, f32 = jnp.bfloat16, jnp.float32
     n_tab = 4
+    n_part = 2
+    step = min(512, vocab_rows)
     sems = pltpu.SemaphoreType.DMA
     vmem = pl.BlockSpec(memory_space=pltpu.VMEM)
     hbm = pl.BlockSpec(memory_space=pl.ANY)
@@ -391,10 +415,10 @@
             pltpu.VMEM((n_t, w_out.shape[0], width), bf16),
             pltpu.VMEM(key_cache.shape[1:], bf16),
             pltpu.VMEM(value_cache.shape[1:], bf16),
-            pltpu.VMEM((n_dp * capacity, width), f32),
-            pltpu.VMEM((n_dp, capacity, width), bf16),
-            pltpu.VMEM((n_dp, capacity, width), bf16),
-            pltpu.VMEM((n_t, nodes, width), bf16),
+            pltpu.VMEM((vocab_rows // step, n_dp * capacity, step), bf16),
+            pltpu.VMEM((n_part, n_dp, capacity, width // n_part), bf16),
+            pltpu.VMEM((n_part, n_dp, capacity, width // n_part), bf16),
+            pltpu.VMEM((n_part, n_t, nodes, width // n_part), bf16),
             pltpu.VMEM((nodes, w_query.shape[1]), bf16),
             pltpu.VMEM((n_chip, nodes, width), bf16),
             pltpu.VMEM((n_chip, nodes, width), bf16),
@@ -405,12 +429,11 @@
             sems((n_t,)),
             sems((n_dp,)),
             sems((n_dp,)),
-            sems((n_dp,)),
-            sems((n_dp,)),
-            sems((1,)),
-            sems((n_chip,)),
-            sems((n_t,)),
-            sems((n_chip,)),
+            sems((n_part, n_dp)),
+            sems((n_part, n_dp)),
+            sems((n_part, n_chip)),
+            sems((n_part, n_t)),
+            sems((n_part, n_chip)),
             sems((n_chip,)),
             sems((n_chip,)),
             sems((n_chip,)),

time: 42.6 us -> 43 us (level)
  no operation moved by 1% of the time
where the time goes in v3:
time: 43 us; the launch traced here: 42.8 us
  Pallas kernels  40.5 us (94%)
  other arithmetic  1.62 us (4%)
  between operations  0.66 us (2%)
    pallas_call x1, Pallas kernels, shards(): pl.pallas_call(functools.partial(layer_kernel, n_dp, n_t, nodes, capacity...  40.5 us
    convert_element_type x1, other arithmetic, shards(): return pl.pallas_call(functools.partial(layer_kernel, n_dp, n_t, nodes, c...  1.62 us

profile of v3, /device:TPU:0, one launch (start us, length us, event | category | flops | bytes accessed | tf_op | source)
XLA Modules:
  0.0 42.8 jit_solution(11553609770717444984)
XLA Ops:
  0.7 40.5 %shard_map.100 = f32[64,1024]{1,0:T(8,128)} custom-call(s32[1,64]{1,0:T(1,128)} %ids_ref.1, s32[1,64,64]{2,1,0:T(8,128)} %anc_ref.1, s32[1]{0:T(128)S(6)} %copy.11.len_ref, bf16[4096]{0:T(1024)(128)(2,1)} %gain_ref.1, bf16[8192,1024]{1,0:T(8,128)(2,1)} %table_hbm.1, bf16[4096,1024]{1,0:T(8,128)(2,1)} %wq_hbm.1, bf16[2,4096,256]{2,1,0:T(8,128)(2,1)} %wkv_hbm.1, ...), custom_call_target="tpu_custom_call" | custom-call | tf_op jit(solution)/shard_map/pallas_call | solution.py:403
  41.2 1.6 %convert_element_type.3 = bf16[64,1024]{1,0:T(8,128)(2,1)} convert(f32[64,1024]{1,0:T(8,128)} %shard_map.100) | non-fusion elementwise | flops 65536 | bytes 393216 | tf_op jit(solution)/shard_map/convert_element_type | solution.py:456

commit v4 on v3

--- a/solution.py
+++ b/solution.py
@@ -39,7 +39,7 @@
     wout_v,
     kc_v,
     vc_v,
-    pick_v,
+    acc,
     slot_send,
     slot_recv,
     emb_all,
@@ -201,29 +201,28 @@
         )
         - 1.0
     ).astype(jnp.int32)
-    step = min(512, vocab_rows)
+    step = min(8192, vocab_rows)
     step_lane = lax.broadcasted_iota(jnp.int32, (slots, step), 1)
-    for i in range(vocab_rows // step):
-        pick_v[i] = ((step_lane + i * step) == offset).astype(jnp.float32).astype(jnp.bfloat16)
     for copy in table_copies:
         copy.wait()
 
+    acc[...] = jnp.zeros_like(acc)
+
+    def table_step(i, carry):
+        first = pl.multiple_of(i * step, step)
+        pick = ((step_lane + first) == offset).astype(jnp.float32).astype(jnp.bfloat16)
+        acc[...] += jnp.dot(
+            pick, table_v[pl.ds(first, step), :], preferred_element_type=jnp.float32
+        )
+        return carry
+
+    lax.fori_loop(0, vocab_rows // step, table_step, 0)
     row_copies = []
     for q in range(n_part):
-
-        def table_step(i, total, q=q):
-            first = pl.multiple_of(i * step, step)
-            return total + jnp.dot(
-                pick_v[i],
-                table_v[pl.ds(first, step), q * part_width : (q + 1) * part_width],
-                preferred_element_type=jnp.float32,
-            )
-
-        picked = lax.fori_loop(
-            0, vocab_rows // step, table_step, jnp.zeros((slots, part_width), jnp.float32)
-        ).astype(jnp.bfloat16)
         for k in range(n_dp):
-            slot_send[q, k] = picked[k * capacity : (k + 1) * capacity, :]
+            slot_send[q, k] = acc[
+                k * capacity : (k + 1) * capacity, q * part_width : (q + 1) * part_width
+            ].astype(jnp.bfloat16)
         for k in range(1, n_dp):
             back = n_dp - k
             copy = dp_copy(
@@ -396,7 +395,6 @@
     bf16, f32 = jnp.bfloat16, jnp.float32
     n_tab = 4
     n_part = 2
-    step = min(512, vocab_rows)
     sems = pltpu.SemaphoreType.DMA
     vmem = pl.BlockSpec(memory_space=pltpu.VMEM)
     hbm = pl.BlockSpec(memory_space=pl.ANY)
@@ -415,7 +413,7 @@
             pltpu.VMEM((n_t, w_out.shape[0], width), bf16),
             pltpu.VMEM(key_cache.shape[1:], bf16),
             pltpu.VMEM(value_cache.shape[1:], bf16),
-            pltpu.VMEM((vocab_rows // step, n_dp * capacity, step), bf16),
+            pltpu.VMEM((n_dp * capacity, width), f32),
             pltpu.VMEM((n_part, n_dp, capacity, width // n_part), bf16),
             pltpu.VMEM((n_part, n_dp, capacity, width // n_part), bf16),
             pltpu.VMEM((n_part, n_t, nodes, width // n_part), bf16),

time: 43 us -> 38.8 us (0.902)
  Pallas kernels: 40.5 us -> 36.3 us
    pallas_call x1, Pallas kernels: 40.5 us -> 36.3 us  [shards(): pl.pallas_call(functools.partial(layer_kernel, n_dp, n_t, nodes, capacity...]
where the time goes in v4:
time: 38.8 us; the launch traced here: 38.6 us
  Pallas kernels  36.3 us (94%)
  other arithmetic  1.62 us (4%)
  between operations  0.66 us (2%)
    pallas_call x1, Pallas kernels, shards(): pl.pallas_call(functools.partial(layer_kernel, n_dp, n_t, nodes, capacity...  36.3 us
    convert_element_type x1, other arithmetic, shards(): return pl.pallas_call(functools.partial(layer_kernel, n_dp, n_t, nodes, c...  1.62 us

profile of v4, /device:TPU:0, one launch (start us, length us, event | category | flops | bytes accessed | tf_op | source)
XLA Modules:
  0.0 38.6 jit_solution(3254512078088954891)
XLA Ops:
  0.7 36.3 %shard_map.100 = f32[64,1024]{1,0:T(8,128)} custom-call(s32[1,64]{1,0:T(1,128)} %ids_ref.1, s32[1,64,64]{2,1,0:T(8,128)} %anc_ref.1, s32[1]{0:T(128)S(6)} %copy.11.len_ref, bf16[4096]{0:T(1024)(128)(2,1)} %gain_ref.1, bf16[8192,1024]{1,0:T(8,128)(2,1)} %table_hbm.1, bf16[4096,1024]{1,0:T(8,128)(2,1)} %wq_hbm.1, bf16[2,4096,256]{2,1,0:T(8,128)(2,1)} %wkv_hbm.1, ...), custom_call_target="tpu_custom_call" | custom-call | tf_op jit(solution)/shard_map/pallas_call | solution.py:401
  37.0 1.6 %convert_element_type.3 = bf16[64,1024]{1,0:T(8,128)(2,1)} convert(f32[64,1024]{1,0:T(8,128)} %shard_map.100) | non-fusion elementwise | flops 65536 | bytes 393216 | tf_op jit(solution)/shard_map/convert_element_type | solution.py:454
